TPU v7x, 32 devices: a whole 2x2x4 slice. The times are simulated.
32 devices in a mesh: grp: 4 (over y, x), row: 2 (over core), col: 4 (over z).
Axes of the slice: x: 2, y: 2, z: 4, core: 2. Of those that a mesh axis runs over, the one named last changes fastest.
Arguments:
- normals: float32 [4, 4096, 4096], P('grp', 'row', 'col'), as said below
- transforms: float32 [4, 32, 128, 128], P('grp', 'row'), as said below
- block_map: int32 [4, 32], P('grp'), may hold values from 0 to 31, as said below
Outputs:
- eliminated: float32 [4096, 4096], P('row', 'col')
Inputs may be any that keep to these rules, and one draw needn't show every extreme that they name: `block_map`: for each group, a permutation of the blocks that maps every aligned range of 8 blocks onto itself. `normals`: each group's matrix is symmetric positive definite. `transforms`: each block is nonsingular.
All inputs are finite; a program needn't handle non-finite values.
Results may differ from a plain program's by a relative error of at most 0.0001.
Values sent between devices are 32-bit elements; how exact they have to be, the bound alone decides.
No kernel may reach another device: no remote copies, remote signals or barrier semaphores. Data moves between devices by JAX's collectives and lax.ppermute only.
A program may use at most 64 MiB of HBM per device.

v0:
```python
import jax
import jax.numpy as jnp
from jax import lax
from jax.sharding import PartitionSpec as P

BLK = 128
NPAN = 5


def spread(block, axis, holder):
    block = jnp.where(lax.axis_index(axis) == holder, block, jnp.zeros_like(block))
    return lax.psum(block, axis)


def on_device(normals, transforms, block_map):
    local = normals[0]
    height, width = local.shape
    row_blocks = height // BLK
    col_blocks = width // BLK
    row_index = lax.axis_index("row")
    col_index = lax.axis_index("col")
    row_transforms = transforms[0]
    every_block = lax.all_gather(transforms, "row", axis=1, tiled=True)[0]
    col_transforms = lax.dynamic_slice_in_dim(every_block, col_index * col_blocks, col_blocks, 0)
    grid = local.reshape(row_blocks, BLK, col_blocks, BLK)
    half_done = jnp.einsum("aij,aibk->ajbk", row_transforms, grid, precision=lax.Precision.HIGHEST)
    rotated = jnp.einsum(
        "ajbk,bkl->ajbl", half_done, col_transforms, precision=lax.Precision.HIGHEST
    )
    mapping = block_map[0]
    row_map = (
        lax.dynamic_slice_in_dim(mapping, row_index * row_blocks, row_blocks, 0)
        - row_index * row_blocks
    )
    col_map = (
        lax.dynamic_slice_in_dim(mapping, col_index * col_blocks, col_blocks, 0)
        - col_index * col_blocks
    )
    rotated = jnp.take(rotated, row_map, axis=0)
    rotated = jnp.take(rotated, col_map, axis=2).reshape(height, width)
    matrix = lax.psum(rotated, "grp")
    row_offset = row_index * height
    own_count = matrix.shape[0]
    order_all = height * lax.axis_size("row")
    col_offset = col_index * width
    for panel in range(NPAN):
        offset = panel * BLK
        holder = offset // width
        inside = offset - holder * width
        panel_piece = spread(matrix[:, inside : inside + BLK], "col", holder)
        column = lax.all_gather(panel_piece, "row", axis=0, tiled=True)
        factor_block = jnp.linalg.cholesky(column[offset : offset + BLK])
        factor = lax.linalg.triangular_solve(
            factor_block, column, left_side=False, lower=True, transpose_a=True
        )
        below = jnp.arange(order_all)[:, None] >= offset
        factor = jnp.where(below, factor, jnp.zeros_like(factor))
        own_rows = lax.dynamic_slice_in_dim(factor, row_offset, own_count, 0)
        col_rows = lax.dynamic_slice_in_dim(factor, col_offset, width, 0)
        matrix = matrix - jnp.dot(
            own_rows,
            col_rows.T,
            precision=lax.Precision.HIGHEST,
            preferred_element_type=jnp.float32,
        )
        current = matrix[:, inside : inside + BLK]
        matrix = matrix.at[:, inside : inside + BLK].set(
            jnp.where(col_index == holder, own_rows, current)
        )
    return matrix


def solution(mesh):
    return jax.shard_map(
        on_device,
        mesh=mesh,
        in_specs=(P("grp", "row", "col"), P("grp", "row", None, None), P("grp", None)),
        out_specs=P("row", "col"),
        check_vma=False,
    )
```

profile of v0, /device:TPU:0, one launch (start us, length us, event | category | flops | bytes accessed | tf_op | source)
XLA Modules:
  0.0 811.8 jit_solution(7198959561113941672)
XLA Ops:
  7.3 9.0 %copy.38 = f32[256,8,8,128]{3,2,1,0:T(8,128)} copy(f32[256,8,8,128]{3,1,2,0:T(8,128)} %bitcast.111) | data formatting | bytes 16777216
  16.7 14.3 %fusion = f32[16,128,8,128]{3,1,0,2:T(8,128)} fusion(f32[16,128,8,128]{3,2,1,0:T(8,128)} %bitcast.108, f32[1,16,128,128]{3,2,1,0:T(8,128)S(1)} %copy-done.4), kind=kOutput, calls=%fused_computation.3 | convolution fusion | flops 3221225472 | bytes 17825792 | tf_op jit(solution)/shard_map/aij,aibk->ajbk/dot_general | solution.py:26
  31.0 12.0 %convolution_bitcast_fusion.5 = f32[16,128,8,128]{1,3,0,2:T(8,128)} fusion(f32[16,128,8,128]{3,1,0,2:T(8,128)} %fusion, f32[1,32,128,128]{3,2,0,1:T(8,128)} %all-gather.7.cloned.1.call-done, s32[]{:T(128)S(6)} %select_n.123), kind=kOutput, calls=%fused_computation.20 | convolution fusion | flops 3221225472 | bytes 17301508 | tf_op jit(solution)/shard_map/ajbk,bkl->ajbl/dot_general | solution.py:27
  43.0 7.7 gather_fusion
  50.7 8.6 %broadcast_select_fusion = f32[16,128,8,128]{1,3,2,0:T(8,128)} fusion(f32[16,128,8,128]{1,3,2,0:T(8,128)} %gather_fusion, pred[16]{0:T(512)(128)(4,1)S(1)} %compare_and_fusion), kind=kLoop, calls=%fused_computation.19 | loop fusion | flops 2097152 | bytes 16777232 | tf_op jit(solution)/shard_map/jit(_take)/select_n | solution.py:39
  59.3 7.7 gather_fusion.1
  67.0 8.1 copy.19
  75.1 7.0 bitcast_select_fusion
  82.2 174.8 %all-reduce.7.cloned.1.call-done = f32[2048,1024]{0,1:T(8,128)} async-done(((f32[2048,1024]{0,1:T(8,128)}), f32[2048,1024]{0,1:T(8,128)}) %all-reduce.7.cloned.1.call-update) | async-done | bytes 8388624 | tf_op jit(solution)/shard_map/psum | solution.py:41
  257.0 2.3 slice_select_fusion.4
  259.4 52.7 %all-reduce.9.cloned.1.call-done = f32[2048,128]{0,1:T(8,128)} async-done(((f32[2048,128]{0,1:T(8,128)}), f32[2048,128]{0,1:T(8,128)}) %all-reduce.9.cloned.1.call-update) | async-done | bytes 1048592 | tf_op jit(solution)/shard_map/psum | solution.py:12
  313.0 10.3 %all-gather.9.cloned.1.call-done = f32[4096,128]{0,1:T(8,128)} async-done(((f32[2048,128]{0,1:T(8,128)}), f32[4096,128]{0,1:T(8,128)}) %all-gather.9.cloned.1.call-update) | async-done | bytes 2097168 | tf_op jit(solution)/shard_map/all_gather | solution.py:51
  325.1 11.7 %cholesky.89 = f32[128,128]{1,0:T(8,128)S(1)} custom-call(f32[128,128]{1,0:T(8,128)S(1)} %fusion.38), custom_call_target="Cholesky" | custom-call | tf_op jit(solution)/shard_map/jit(cholesky)/cholesky | solution.py:52
  338.2 9.8 %custom-call.9 = f32[1,128,128]{1,2,0:T(8,128)S(1)} custom-call(f32[1,128,128]{2,1,0:T(8,128)S(1)} %fusion.24), custom_call_target="InvertDiagBlocksLowerTriangular" | custom-call | tf_op jit(solution)/shard_map/triangular_solve/custom-call.0 | solution.py:53
  348.0 3.5 convolution_bitcast_fusion.4
  351.5 9.4 %convolution_subtract_fusion.4 = f32[2048,1024]{0,1:T(8,128)S(1)} fusion(f32[2048,1024]{0,1:T(8,128)} %all-reduce.7.cloned.1.call-done, f32[4096,128]{0,1:T(8,128)S(1)} %convolution_bitcast_fusion.4, s32[]{:T(128)S(6)} %select_n.133, s32[]{:T(128)S(6)} %select_n.134), kind=kOutput, calls=%fused_computation.18 | convolution fusion | flops 3223322624 | bytes 18350088 | tf_op jit(solution)/shard_map/dot_general | solution.py:60
  361.9 3.4 copy-done
  365.2 1.1 slice_select_fusion.3
  366.4 53.2 %all-reduce.11.cloned.1.call-done = f32[2048,128]{0,1:T(8,128)} async-done(((f32[2048,128]{0,1:T(8,128)}), f32[2048,128]{0,1:T(8,128)}) %all-reduce.11.cloned.1.call-update) | async-done | bytes 1048592 | tf_op jit(solution)/shard_map/psum | solution.py:12
  419.6 1.1 compare_reduce_fusion.8
  420.7 10.1 %all-gather.11.cloned.1.call-done = f32[4096,128]{0,1:T(8,128)} async-done(((f32[2048,128]{0,1:T(8,128)}), f32[4096,128]{0,1:T(8,128)}) %all-gather.11.cloned.1.call-update) | async-done | bytes 2097168 | tf_op jit(solution)/shard_map/all_gather | solution.py:51
  432.6 11.7 %cholesky.100 = f32[128,128]{1,0:T(8,128)S(1)} custom-call(f32[128,128]{1,0:T(8,128)S(1)} %fusion.36), custom_call_target="Cholesky" | custom-call | tf_op jit(solution)/shard_map/jit(cholesky)/cholesky | solution.py:52
  445.7 9.8 %custom-call.10 = f32[1,128,128]{1,2,0:T(8,128)S(1)} custom-call(f32[1,128,128]{2,1,0:T(8,128)S(1)} %fusion.25), custom_call_target="InvertDiagBlocksLowerTriangular" | custom-call | tf_op jit(solution)/shard_map/triangular_solve/custom-call.0 | solution.py:53
  455.5 3.5 fusion.5
  459.0 9.4 %convolution_subtract_fusion.3 = f32[2048,1024]{0,1:T(8,128)S(1)} fusion(f32[2048,1024]{0,1:T(8,128)} %copy-done, f32[4096,128]{0,1:T(8,128)S(1)} %fusion.5, s32[]{:T(128)S(6)} %select_n.133, s32[]{:T(128)S(6)} %select_n.134), kind=kOutput, calls=%fused_computation.17 | convolution fusion | flops 3223322624 | bytes 18350088 | tf_op jit(solution)/shard_map/dot_general | solution.py:60
  469.3 3.4 copy-done.1
  473.8 53.2 %all-reduce.13.cloned.1.call-done = f32[2048,128]{0,1:T(8,128)} async-done(((f32[2048,128]{0,1:T(8,128)}), f32[2048,128]{0,1:T(8,128)}) %all-reduce.13.cloned.1.call-update) | async-done | bytes 1048592 | tf_op jit(solution)/shard_map/psum | solution.py:12
  527.9 10.6 %all-gather.13.cloned.1.call-done = f32[4096,128]{0,1:T(8,128)} async-done(((f32[2048,128]{0,1:T(8,128)}), f32[4096,128]{0,1:T(8,128)}) %all-gather.13.cloned.1.call-update) | async-done | bytes 2097168 | tf_op jit(solution)/shard_map/all_gather | solution.py:51
  540.2 11.7 %cholesky.111 = f32[128,128]{1,0:T(8,128)S(1)} custom-call(f32[128,128]{1,0:T(8,128)S(1)} %fusion.34), custom_call_target="Cholesky" | custom-call | tf_op jit(solution)/shard_map/jit(cholesky)/cholesky | solution.py:52
  553.2 9.8 %custom-call.11 = f32[1,128,128]{1,2,0:T(8,128)S(1)} custom-call(f32[1,128,128]{2,1,0:T(8,128)S(1)} %fusion.26), custom_call_target="InvertDiagBlocksLowerTriangular" | custom-call | tf_op jit(solution)/shard_map/triangular_solve/custom-call.0 | solution.py:53
  563.1 3.5 fusion.4
  566.6 9.4 %convolution_subtract_fusion.2 = f32[2048,1024]{0,1:T(8,128)S(1)} fusion(f32[2048,1024]{0,1:T(8,128)} %copy-done.1, f32[4096,128]{0,1:T(8,128)S(1)} %fusion.4, s32[]{:T(128)S(6)} %select_n.133, s32[]{:T(128)S(6)} %select_n.134), kind=kOutput, calls=%fused_computation.16 | convolution fusion | flops 3223322624 | bytes 18350088 | tf_op jit(solution)/shard_map/dot_general | solution.py:60
  576.9 3.4 copy-done.2
  581.8 52.8 %all-reduce.15.cloned.1.call-done = f32[2048,128]{0,1:T(8,128)} async-done(((f32[2048,128]{0,1:T(8,128)}), f32[2048,128]{0,1:T(8,128)}) %all-reduce.15.cloned.1.call-update) | async-done | bytes 1048592 | tf_op jit(solution)/shard_map/psum | solution.py:12
  635.3 10.6 %all-gather.15.cloned.1.call-done = f32[4096,128]{0,1:T(8,128)} async-done(((f32[2048,128]{0,1:T(8,128)}), f32[4096,128]{0,1:T(8,128)}) %all-gather.15.cloned.1.call-update) | async-done | bytes 2097168 | tf_op jit(solution)/shard_map/all_gather | solution.py:51
  647.6 11.7 %cholesky.122 = f32[128,128]{1,0:T(8,128)S(1)} custom-call(f32[128,128]{1,0:T(8,128)S(1)} %fusion.32), custom_call_target="Cholesky" | custom-call | tf_op jit(solution)/shard_map/jit(cholesky)/cholesky | solution.py:52
  660.7 9.8 %custom-call.12 = f32[1,128,128]{1,2,0:T(8,128)S(1)} custom-call(f32[1,128,128]{2,1,0:T(8,128)S(1)} %fusion.27), custom_call_target="InvertDiagBlocksLowerTriangular" | custom-call | tf_op jit(solution)/shard_map/triangular_solve/custom-call.0 | solution.py:53
  670.5 3.5 fusion.3
  674.0 9.4 %convolution_subtract_fusion.1 = f32[2048,1024]{0,1:T(8,128)S(1)} fusion(f32[2048,1024]{0,1:T(8,128)} %copy-done.2, f32[4096,128]{0,1:T(8,128)S(1)} %fusion.3, s32[]{:T(128)S(6)} %select_n.133, s32[]{:T(128)S(6)} %select_n.134), kind=kOutput, calls=%fused_computation.15 | convolution fusion | flops 3223322624 | bytes 18350088 | tf_op jit(solution)/shard_map/dot_general | solution.py:60
  684.3 3.4 copy-done.3
  689.0 53.0 %all-reduce.17.cloned.1.call-done = f32[2048,128]{0,1:T(8,128)} async-done(((f32[2048,128]{0,1:T(8,128)}), f32[2048,128]{0,1:T(8,128)}) %all-reduce.17.cloned.1.call-update) | async-done | bytes 1048592 | tf_op jit(solution)/shard_map/psum | solution.py:12
  742.7 10.6 %all-gather.17.cloned.1.call-done = f32[4096,128]{0,1:T(8,128)} async-done(((f32[2048,128]{0,1:T(8,128)}), f32[4096,128]{0,1:T(8,128)}) %all-gather.17.cloned.1.call-update) | async-done | bytes 2097168 | tf_op jit(solution)/shard_map/all_gather | solution.py:51
  755.1 11.7 %cholesky.133 = f32[128,128]{1,0:T(8,128)S(1)} custom-call(f32[128,128]{1,0:T(8,128)S(1)} %fusion.30), custom_call_target="Cholesky" | custom-call | tf_op jit(solution)/shard_map/jit(cholesky)/cholesky | solution.py:52
  768.1 9.8 %custom-call.13 = f32[1,128,128]{1,2,0:T(8,128)S(1)} custom-call(f32[1,128,128]{2,1,0:T(8,128)S(1)} %fusion.28), custom_call_target="InvertDiagBlocksLowerTriangular" | custom-call | tf_op jit(solution)/shard_map/triangular_solve/custom-call.0 | solution.py:53
  777.9 3.5 fusion.2
  781.5 11.2 %convolution_subtract_fusion = f32[2048,1024]{0,1:T(8,128)} fusion(f32[2048,1024]{0,1:T(8,128)} %copy-done.3, f32[4096,128]{0,1:T(8,128)S(1)} %fusion.2, s32[]{:T(128)S(6)} %select_n.133, s32[]{:T(128)S(6)} %select_n.134), kind=kOutput, calls=%fused_computation.14 | convolution fusion | flops 3223322624 | bytes 18350088 | tf_op jit(solution)/shard_map/dot_general | solution.py:60
  792.6 2.9 fusion.10
  795.5 9.2 %copy.30 = f32[2048,1024]{1,0:T(8,128)} copy(f32[2048,1024]{0,1:T(8,128)} %fusion.10) | data formatting | bytes 16777216 | tf_op jit(solution)/shard_map/scatter | solution.py:67
  (85 shorter events, 27.5 us)
Async XLA Ops:
  6.5 24.5 %all-gather.7.cloned.1.call-start = ((), (), s32[]{:S(2)}) async-start(), calls=%async_computation | async-start | bytes 3145728 | tf_op jit(solution)/shard_map/all_gather | solution.py:23
  7.3 249.7 %all-reduce.7.cloned.1.call-start = ((), (), s32[]{:S(2)}) async-start(), calls=%async_computation.1 | async-start | bytes 16777216 | tf_op jit(solution)/shard_map/psum | solution.py:41
  7.3 9.0 %copy-start.5 = (s32[1,32]{1,0:T(1,128)S(1)}, s32[1,32]{1,0:T(1,128)}, u32[]{:S(2)}) copy-start(s32[1,32]{1,0:T(1,128)} %param.18) | copy-start | bytes 388
  7.3 9.4 %copy-start.4 = (f32[1,16,128,128]{3,2,1,0:T(8,128)S(1)}, f32[1,16,128,128]{3,2,1,0:T(8,128)}, u32[]{:S(2)}) copy-start(f32[1,16,128,128]{3,2,1,0:T(8,128)} %param.17) | copy-start | bytes 3145732
  82.1 229.9 %all-reduce.9.cloned.1.call-start = ((), (), s32[]{:S(2)}) async-start(), calls=%async_computation.2 | async-start | bytes 2097152 | tf_op jit(solution)/shard_map/psum | solution.py:12
  259.3 64.0 %all-gather.9.cloned.1.call-start = ((), (), s32[]{:S(2)}) async-start(), calls=%async_computation.3 | async-start | bytes 3145728 | tf_op jit(solution)/shard_map/all_gather | solution.py:51
  312.1 107.5 %all-reduce.11.cloned.1.call-start = ((), (), s32[]{:S(2)}) async-start(), calls=%async_computation.4 | async-start | bytes 2097152 | tf_op jit(solution)/shard_map/psum | solution.py:12
  361.8 3.4 copy-start
  366.3 64.5 %all-gather.11.cloned.1.call-start = ((), (), s32[]{:S(2)}) async-start(), calls=%async_computation.5 | async-start | bytes 3145728 | tf_op jit(solution)/shard_map/all_gather | solution.py:51
  419.6 107.4 %all-reduce.13.cloned.1.call-start = ((), (), s32[]{:S(2)}) async-start(), calls=%async_computation.6 | async-start | bytes 2097152 | tf_op jit(solution)/shard_map/psum | solution.py:12
  469.3 3.4 copy-start.1
  473.8 64.6 %all-gather.13.cloned.1.call-start = ((), (), s32[]{:S(2)}) async-start(), calls=%async_computation.7 | async-start | bytes 3145728 | tf_op jit(solution)/shard_map/all_gather | solution.py:51
  527.0 107.6 %all-reduce.15.cloned.1.call-start = ((), (), s32[]{:S(2)}) async-start(), calls=%async_computation.8 | async-start | bytes 2097152 | tf_op jit(solution)/shard_map/psum | solution.py:12
  576.9 3.4 copy-start.2
  581.3 64.5 %all-gather.15.cloned.1.call-start = ((), (), s32[]{:S(2)}) async-start(), calls=%async_computation.9 | async-start | bytes 3145728 | tf_op jit(solution)/shard_map/all_gather | solution.py:51
  634.6 107.4 %all-reduce.17.cloned.1.call-start = ((), (), s32[]{:S(2)}) async-start(), calls=%async_computation.10 | async-start | bytes 2097152 | tf_op jit(solution)/shard_map/psum | solution.py:12
  684.3 3.4 copy-start.3
  688.8 64.5 %all-gather.17.cloned.1.call-start = ((), (), s32[]{:S(2)}) async-start(), calls=%async_computation.11 | async-start | bytes 3145728 | tf_op jit(solution)/shard_map/all_gather | solution.py:51
Sparse Core Ops, SparseCore 0:
  8.9 13.3 all-gather.6
  82.2 174.7 all-reduce.6
  259.4 52.5 all-reduce.8
  313.4 9.8 all-gather.8
  366.5 53.0 all-reduce.10
  421.0 9.8 all-gather.10
  473.9 53.0 all-reduce.12
  528.5 9.8 all-gather.12
  581.5 53.0 all-reduce.14
  636.0 9.8 all-gather.14
  688.9 53.0 all-reduce.16
  743.4 9.8 all-gather.16
where the time goes:
time: 821 us; the launch traced here: 812 us
  waiting for transfers between devices  493 us (60%)
  other arithmetic  151 us (18%)
  matrix products  92.7 us (11%)
  local copies, waits for them, and re-layouts  60 us (7%)
  between operations  14.1 us (2%)
    psum x5, waiting for transfers between devices, spread(): return lax.psum(block, axis)  265 us
    psum x1, waiting for transfers between devices, on_device(): matrix = lax.psum(rotated, 'grp')  175 us
    another operation x15, other arithmetic, on_device(): factor_block = jnp.linalg.cholesky(column[offset:offset + BLK])  62 us
    another operation x10, other arithmetic, on_device(): lax.linalg.triangular_solve(factor_block, column, left_side=False, lower=...  52.2 us
    all_gather x5, waiting for transfers between devices, on_device(): column = lax.all_gather(panel_piece, 'row', axis=0, tiled=True)  52.2 us
    dot_general x5, matrix products, on_device(): jnp.dot(own_rows, col_rows.T, precision=lax.Precision.HIGHEST, preferred_...  48.8 us
    unnamed x13, local copies, waits for them, and re-layouts  22.5 us
    another operation x5, matrix products, on_device(): lax.linalg.triangular_solve(factor_block, column, left_side=False, lower=...  17.5 us
  transfers between devices with their start and end apart: 12, of which 11 were waited for; matrix products, arithmetic and copies ran while one was open for 3% of the time, Pallas kernels for 0%

commit v1 on v0

--- a/solution.py
+++ b/solution.py
@@ -2,6 +2,7 @@
 import jax.numpy as jnp
 from jax import lax
 from jax.sharding import PartitionSpec as P
+from jax.lax import ppermute, psum
 
 BLK = 128
 NPAN = 5
@@ -38,7 +39,14 @@
     )
     rotated = jnp.take(rotated, row_map, axis=0)
     rotated = jnp.take(rotated, col_map, axis=2).reshape(height, width)
-    matrix = lax.psum(rotated, "grp")
+    matrix = rotated
+    p_count = psum(1, "grp")
+    for to_i in [jj for jj in (1, 2, 4, 8, 16) if jj < p_count]:
+        xs_all = []
+        for p in range(p_count):
+            xs_all.append((p, p ^ to_i))
+        view_out = ppermute(matrix, "grp", xs_all)
+        matrix = matrix + view_out
     row_offset = row_index * height
     own_count = matrix.shape[0]
     order_all = height * lax.axis_size("row")

time: 821 us -> 1040 us (1.27)
  waiting for transfers between devices: 493 us -> 680 us
  other arithmetic: 151 us -> 168 us
  matrix products: 92.7 us -> 104 us
    ppermute x0 -> x2, waiting for transfers between devices: none -> 361 us  [on_device(): view_out = ppermute(matrix, 'grp', xs_all)]
    psum x1 -> x0, waiting for transfers between devices: 175 us -> none  [on_device(): matrix = lax.psum(rotated, 'grp')]
    add x0 -> x2, other arithmetic: none -> 19.4 us  [on_device(): matrix = matrix + view_out]
    dot_general x1, matrix products: 12 us -> 23.6 us  [on_device(): jnp.einsum('ajbk,bkl->ajbl', half_done, col_transforms, precision=lax.Pre...]
  transfers between devices with their start and end apart: 12 -> 13, of which waited for: 11 -> 12; matrix products, arithmetic and copies ran while one was open for 3% -> 3% of each run, Pallas kernels for 0% -> 0%
where the time goes in v1:
time: 1040 us; the launch traced here: 1030 us
  waiting for transfers between devices  680 us (65%)
  other arithmetic  168 us (16%)
  matrix products  104 us (10%)
  local copies, waits for them, and re-layouts  60 us (6%)
  between operations  13.8 us (1%)
    ppermute x2, waiting for transfers between devices, on_device(): view_out = ppermute(matrix, 'grp', xs_all)  361 us
    psum x5, waiting for transfers between devices, spread(): return lax.psum(block, axis)  265 us
    another operation x15, other arithmetic, on_device(): factor_block = jnp.linalg.cholesky(column[offset:offset + BLK])  62 us
    all_gather x5, waiting for transfers between devices, on_device(): column = lax.all_gather(panel_piece, 'row', axis=0, tiled=True)  53 us
    another operation x10, other arithmetic, on_device(): lax.linalg.triangular_solve(factor_block, column, left_side=False, lower=...  52.2 us
    dot_general x5, matrix products, on_device(): jnp.dot(own_rows, col_rows.T, precision=lax.Precision.HIGHEST, preferred_...  48.8 us
    dot_general x1, matrix products, on_device(): jnp.einsum('ajbk,bkl->ajbl', half_done, col_transforms, precision=lax.Pre...  23.6 us
    unnamed x13, local copies, waits for them, and re-layouts  22.5 us
  transfers between devices with their start and end apart: 13, of which 12 were waited for; matrix products, arithmetic and copies ran while one was open for 3% of the time, Pallas kernels for 0%

profile of v1, /device:TPU:0, one launch (start us, length us, event | category | flops | bytes accessed | tf_op | source)
XLA Modules:
  0.0 1031.8 jit_solution(8755545976372448167)
XLA Ops:
  7.3 9.0 copy.38
  16.7 14.3 %fusion = f32[16,128,8,128]{3,1,0,2:T(8,128)} fusion(f32[16,128,8,128]{3,2,1,0:T(8,128)} %bitcast.112, f32[1,16,128,128]{3,2,1,0:T(8,128)S(1)} %copy-done.4), kind=kOutput, calls=%fused_computation.3 | convolution fusion | flops 3221225472 | bytes 17825792 | tf_op jit(solution)/shard_map/aij,aibk->ajbk/dot_general | solution.py:27
  31.0 23.6 %convolution_bitcast_fusion.5 = f32[16,128,8,128]{1,3,0,2:T(8,128)} fusion(f32[16,128,8,128]{3,1,0,2:T(8,128)} %fusion, f32[1,32,128,128]{3,2,0,1:T(8,128)} %all-gather.7.cloned.1.call-done, s32[]{:T(128)S(6)} %select_n.123), kind=kOutput, calls=%fused_computation.20 | convolution fusion | flops 3221225472 | bytes 17301508 | tf_op jit(solution)/shard_map/ajbk,bkl->ajbl/dot_general | solution.py:28
  54.6 7.7 gather_fusion
  62.3 8.6 broadcast_select_fusion
  70.8 7.7 gather_fusion.1
  78.5 8.1 copy.19
  86.7 4.8 bitcast_select_fusion
  91.5 3.1 collective-permute-start
  94.6 180.4 %collective-permute-done = f32[2048,1024]{0,1:T(8,128)S(1)} collective-permute-done((f32[2048,1024]{0,1:T(8,128)S(1)}, f32[2048,1024]{0,1:T(8,128)S(1)}, u32[]{:S(2)}, u32[]{:S(2)}) %collective-permute-start) | collective-permute-done | bytes 8388640 | tf_op jit(solution)/shard_map/ppermute | solution.py:48
  275.0 7.5 fusion.55
  284.3 180.1 %collective-permute-done.1 = f32[2048,1024]{0,1:T(8,128)} collective-permute-done((f32[2048,1024]{0,1:T(8,128)}, f32[2048,1024]{0,1:T(8,128)}, u32[]{:S(2)}, u32[]{:S(2)}) %collective-permute-start.1) | collective-permute-done | bytes 8388640 | tf_op jit(solution)/shard_map/ppermute | solution.py:48
  464.4 11.9 %add.92 = f32[2048,1024]{0,1:T(8,128)} add(f32[2048,1024]{0,1:T(8,128)} %fusion.55, f32[2048,1024]{0,1:T(8,128)} %collective-permute-done.1) | non-fusion elementwise | flops 2097152 | bytes 25165824 | tf_op jit(solution)/shard_map/add | solution.py:49
  478.7 53.3 %all-reduce.6.cloned.1.call-done = f32[2048,128]{0,1:T(8,128)} async-done(((f32[2048,128]{0,1:T(8,128)}), f32[2048,128]{0,1:T(8,128)}) %all-reduce.6.cloned.1.call-update) | async-done | bytes 1048592 | tf_op jit(solution)/shard_map/psum | solution.py:13
  533.1 10.3 %all-gather.9.cloned.1.call-done = f32[4096,128]{0,1:T(8,128)} async-done(((f32[2048,128]{0,1:T(8,128)}), f32[4096,128]{0,1:T(8,128)}) %all-gather.9.cloned.1.call-update) | async-done | bytes 2097168 | tf_op jit(solution)/shard_map/all_gather | solution.py:59
  545.2 11.7 %cholesky.89 = f32[128,128]{1,0:T(8,128)S(1)} custom-call(f32[128,128]{1,0:T(8,128)S(1)} %fusion.38), custom_call_target="Cholesky" | custom-call | tf_op jit(solution)/shard_map/jit(cholesky)/cholesky | solution.py:60
  558.3 9.8 custom-call.9
  568.1 3.5 convolution_bitcast_fusion.4
  571.6 9.4 convolution_subtract_fusion.4
  581.9 3.4 copy-done
  586.4 53.2 %all-reduce.8.cloned.1.call-done = f32[2048,128]{0,1:T(8,128)} async-done(((f32[2048,128]{0,1:T(8,128)}), f32[2048,128]{0,1:T(8,128)}) %all-reduce.8.cloned.1.call-update) | async-done | bytes 1048592 | tf_op jit(solution)/shard_map/psum | solution.py:13
  640.4 10.4 %all-gather.11.cloned.1.call-done = f32[4096,128]{0,1:T(8,128)} async-done(((f32[2048,128]{0,1:T(8,128)}), f32[4096,128]{0,1:T(8,128)}) %all-gather.11.cloned.1.call-update) | async-done | bytes 2097168 | tf_op jit(solution)/shard_map/all_gather | solution.py:59
  652.6 11.7 %cholesky.100 = f32[128,128]{1,0:T(8,128)S(1)} custom-call(f32[128,128]{1,0:T(8,128)S(1)} %fusion.36), custom_call_target="Cholesky" | custom-call | tf_op jit(solution)/shard_map/jit(cholesky)/cholesky | solution.py:60
  665.7 9.8 custom-call.10
  675.5 3.5 fusion.5
  679.0 9.4 convolution_subtract_fusion.3
  689.3 3.4 copy-done.1
  694.2 52.8 %all-reduce.10.cloned.1.call-done = f32[2048,128]{0,1:T(8,128)} async-done(((f32[2048,128]{0,1:T(8,128)}), f32[2048,128]{0,1:T(8,128)}) %all-reduce.10.cloned.1.call-update) | async-done | bytes 1048592 | tf_op jit(solution)/shard_map/psum | solution.py:13
  747.7 10.7 %all-gather.13.cloned.1.call-done = f32[4096,128]{0,1:T(8,128)} async-done(((f32[2048,128]{0,1:T(8,128)}), f32[4096,128]{0,1:T(8,128)}) %all-gather.13.cloned.1.call-update) | async-done | bytes 2097168 | tf_op jit(solution)/shard_map/all_gather | solution.py:59
  760.2 11.7 %cholesky.111 = f32[128,128]{1,0:T(8,128)S(1)} custom-call(f32[128,128]{1,0:T(8,128)S(1)} %fusion.34), custom_call_target="Cholesky" | custom-call | tf_op jit(solution)/shard_map/jit(cholesky)/cholesky | solution.py:60
  773.2 9.8 custom-call.11
  783.0 3.5 fusion.4
  786.6 9.4 convolution_subtract_fusion.2
  796.8 3.4 copy-done.2
  801.6 53.0 %all-reduce.12.cloned.1.call-done = f32[2048,128]{0,1:T(8,128)} async-done(((f32[2048,128]{0,1:T(8,128)}), f32[2048,128]{0,1:T(8,128)}) %all-reduce.12.cloned.1.call-update) | async-done | bytes 1048592 | tf_op jit(solution)/shard_map/psum | solution.py:13
  855.2 10.7 %all-gather.15.cloned.1.call-done = f32[4096,128]{0,1:T(8,128)} async-done(((f32[2048,128]{0,1:T(8,128)}), f32[4096,128]{0,1:T(8,128)}) %all-gather.15.cloned.1.call-update) | async-done | bytes 2097168 | tf_op jit(solution)/shard_map/all_gather | solution.py:59
  867.8 11.7 %cholesky.122 = f32[128,128]{1,0:T(8,128)S(1)} custom-call(f32[128,128]{1,0:T(8,128)S(1)} %fusion.32), custom_call_target="Cholesky" | custom-call | tf_op jit(solution)/shard_map/jit(cholesky)/cholesky | solution.py:60
  880.8 9.8 custom-call.12
  890.6 3.5 fusion.3
  894.1 9.4 convolution_subtract_fusion.1
  904.4 3.4 copy-done.3
  909.2 53.0 %all-reduce.14.cloned.1.call-done = f32[2048,128]{0,1:T(8,128)} async-done(((f32[2048,128]{0,1:T(8,128)}), f32[2048,128]{0,1:T(8,128)}) %all-reduce.14.cloned.1.call-update) | async-done | bytes 1048592 | tf_op jit(solution)/shard_map/psum | solution.py:13
  962.8 10.8 %all-gather.17.cloned.1.call-done = f32[4096,128]{0,1:T(8,128)} async-done(((f32[2048,128]{0,1:T(8,128)}), f32[4096,128]{0,1:T(8,128)}) %all-gather.17.cloned.1.call-update) | async-done | bytes 2097168 | tf_op jit(solution)/shard_map/all_gather | solution.py:59
  975.4 11.7 %cholesky.133 = f32[128,128]{1,0:T(8,128)S(1)} custom-call(f32[128,128]{1,0:T(8,128)S(1)} %fusion.30), custom_call_target="Cholesky" | custom-call | tf_op jit(solution)/shard_map/jit(cholesky)/cholesky | solution.py:60
  988.4 9.8 custom-call.13
  998.2 3.5 fusion.2
  1001.7 11.2 %convolution_subtract_fusion = f32[2048,1024]{0,1:T(8,128)} fusion(f32[2048,1024]{0,1:T(8,128)} %copy-done.3, f32[4096,128]{0,1:T(8,128)S(1)} %fusion.2, s32[]{:T(128)S(6)} %select_n.133, s32[]{:T(128)S(6)} %select_n.134), kind=kOutput, calls=%fused_computation.14 | convolution fusion | flops 3223322624 | bytes 18350088 | tf_op jit(solution)/shard_map/dot_general | solution.py:68
  1015.8 9.2 copy.30
  (88 shorter events, 36.3 us)
Async XLA Ops:
  6.5 24.5 %all-gather.7.cloned.1.call-start = ((), (), s32[]{:S(2)}) async-start(), calls=%async_computation | async-start | bytes 3145728 | tf_op jit(solution)/shard_map/all_gather | solution.py:24
  7.3 524.7 %all-reduce.6.cloned.1.call-start = ((), (), s32[]{:S(2)}) async-start(), calls=%async_computation.1 | async-start | bytes 2097152 | tf_op jit(solution)/shard_map/psum | solution.py:13
  7.3 9.0 copy-start.5
  7.3 9.4 copy-start.4
  91.5 183.5 %collective-permute-start = (f32[2048,1024]{0,1:T(8,128)S(1)}, f32[2048,1024]{0,1:T(8,128)S(1)}, u32[]{:S(2)}, u32[]{:S(2)}) collective-permute-start(f32[2048,1024]{0,1:T(8,128)S(1)} %bitcast_select_fusion), channel_id=1, source_target_pairs={{0,8},{8,0},{16,24},{24,16},{1,9},{9,1},{17,25},{25,17},{2,10},{10... | collective-permute-start | bytes 25165832 | tf_op jit(solution)/shard_map/ppermute | solution.py:48
  282.5 181.9 %collective-permute-start.1 = (f32[2048,1024]{0,1:T(8,128)}, f32[2048,1024]{0,1:T(8,128)}, u32[]{:S(2)}, u32[]{:S(2)}) collective-permute-start(f32[2048,1024]{0,1:T(8,128)} %fusion.55), channel_id=1, source_target_pairs={{0,16},{8,24},{16,0},{24,8},{1,17},{9,25},{17,1},{25,9},{2,18},{10... | collective-permute-start | bytes 25165832 | tf_op jit(solution)/shard_map/ppermute | solution.py:48
  478.6 64.8 %all-gather.9.cloned.1.call-start = ((), (), s32[]{:S(2)}) async-start(), calls=%async_computation.2 | async-start | bytes 3145728 | tf_op jit(solution)/shard_map/all_gather | solution.py:59
  532.0 107.5 %all-reduce.8.cloned.1.call-start = ((), (), s32[]{:S(2)}) async-start(), calls=%async_computation.3 | async-start | bytes 2097152 | tf_op jit(solution)/shard_map/psum | solution.py:13
  581.9 3.4 copy-start
  586.4 64.5 %all-gather.11.cloned.1.call-start = ((), (), s32[]{:S(2)}) async-start(), calls=%async_computation.4 | async-start | bytes 3145728 | tf_op jit(solution)/shard_map/all_gather | solution.py:59
  639.6 107.4 %all-reduce.10.cloned.1.call-start = ((), (), s32[]{:S(2)}) async-start(), calls=%async_computation.5 | async-start | bytes 2097152 | tf_op jit(solution)/shard_map/psum | solution.py:13
  689.3 3.4 copy-start.1
  693.8 64.6 %all-gather.13.cloned.1.call-start = ((), (), s32[]{:S(2)}) async-start(), calls=%async_computation.6 | async-start | bytes 3145728 | tf_op jit(solution)/shard_map/all_gather | solution.py:59
  747.0 107.5 %all-reduce.12.cloned.1.call-start = ((), (), s32[]{:S(2)}) async-start(), calls=%async_computation.7 | async-start | bytes 2097152 | tf_op jit(solution)/shard_map/psum | solution.py:13
  796.8 3.4 copy-start.2
  801.3 64.6 %all-gather.15.cloned.1.call-start = ((), (), s32[]{:S(2)}) async-start(), calls=%async_computation.8 | async-start | bytes 3145728 | tf_op jit(solution)/shard_map/all_gather | solution.py:59
  854.6 107.6 %all-reduce.14.cloned.1.call-start = ((), (), s32[]{:S(2)}) async-start(), calls=%async_computation.9 | async-start | bytes 2097152 | tf_op jit(solution)/shard_map/psum | solution.py:13
  904.4 3.4 copy-start.3
  908.9 64.7 %all-gather.17.cloned.1.call-start = ((), (), s32[]{:S(2)}) async-start(), calls=%async_computation.10 | async-start | bytes 3145728 | tf_op jit(solution)/shard_map/all_gather | solution.py:59
Sparse Core Ops, SparseCore 0:
  8.9 13.3 all-gather.6
  478.7 53.2 all-reduce.5
  533.5 9.8 all-gather.8
  586.5 53.0 all-reduce.7
  641.0 9.8 all-gather.10
  693.9 53.0 all-reduce.9
  748.5 9.8 all-gather.12
  801.5 53.0 all-reduce.11
  856.1 9.8 all-gather.14
  909.0 53.0 all-reduce.13
  963.7 9.8 all-gather.16
